TPU v7x, 256 devices: a whole 4x4x8 slice. The times are simulated.
256 devices in a mesh: img: 64 (over x, z, core), grp: 4 (over y).
Axes of the slice: x: 4, y: 4, z: 8, core: 2. Of those that a mesh axis runs over, the one named last changes fastest.
Arguments:
- desc: bfloat16 [256, 1024, 256], P(('img', 'grp')), may hold values from -20 to 20
- w_proj: bfloat16 [256, 512], replicated, may hold values from -0.375 to 0.375
- w_out: bfloat16 [256, 256], replicated, may hold values from -0.375 to 0.375
- pair_list: int32 [1280, 2], P(('img', 'grp')), may hold values from 0 to 255, as said below
- pair_count: int32 [256], P(('img', 'grp')), may hold values from 1 to 5, as said below
Outputs:
- updated: bfloat16 [256, 1024, 256], P(('img', 'grp'))
Inputs may be any that keep to these rules, and one draw needn't show every extreme that they name: `pair_list`: for a slot of the device at img index i, the first image lies in column i (ids i * 4 to i * 4 + 3) and the second in column i or column (i + 1) % 64, and the two ids differ; every slot holds such a pair, live or not. `pair_count`: some device has all 5 slots live.
All inputs are finite; a program needn't handle non-finite values.
Results may differ from a plain program's by a relative error of at most 0.0072.
Values may be sent and summed in bfloat16 or wider, within the bound.
No kernel may reach another device: no remote copies, remote signals or barrier semaphores. Data moves between devices by JAX's collectives and lax.ppermute only.
A program may use at most 64 MiB of HBM per device.

v0:
```python
import jax
import jax.numpy as jnp
from jax import lax
from jax.sharding import PartitionSpec as P

D = 256
HEADS = 4
HEAD_DIM = 64


def from_behind(block, axis, distance):
    devices = range(lax.axis_size(axis))
    route = [((i - distance) % len(devices), i) for i in devices]
    return lax.ppermute(block, axis, route)


def pair_messages(first_rows, second_rows):
    to_first = []
    to_second = []
    for head_index in range(HEADS):
        lower = head_index * HEAD_DIM
        query_first = first_rows[:, lower : lower + HEAD_DIM]
        query_second = second_rows[:, lower : lower + HEAD_DIM]
        value_first = first_rows[:, D + lower : D + lower + HEAD_DIM]
        value_second = second_rows[:, D + lower : D + lower + HEAD_DIM]
        scores = jnp.dot(
            query_first, query_second.T, preferred_element_type=jnp.float32
        ) * HEAD_DIM ** (-0.5)
        across = jnp.exp(scores - jnp.max(scores, axis=1, keepdims=True))
        across = (across / jnp.sum(across, axis=1, keepdims=True)).astype(jnp.bfloat16)
        downward = jnp.exp(scores - jnp.max(scores, axis=0, keepdims=True))
        downward = (downward / jnp.sum(downward, axis=0, keepdims=True)).astype(jnp.bfloat16)
        to_first.append(jnp.dot(across, value_second, preferred_element_type=jnp.float32))
        to_second.append(
            lax.dot_general(
                downward, value_first, (((0,), (0,)), ((), ())), preferred_element_type=jnp.float32
            )
        )
    return (
        jnp.concatenate(to_first, 1).astype(jnp.bfloat16),
        jnp.concatenate(to_second, 1).astype(jnp.bfloat16),
    )


def window_slot(image_ids, column_index, columns, members):
    return (image_ids // members - column_index) % columns * members + image_ids % members


def on_device(desc, w_proj, w_out, pair_list, pair_count):
    columns = lax.axis_size("img")
    members = lax.axis_size("grp")
    column_index = lax.axis_index("img")
    keypoints = desc.shape[1]
    own_rows = jnp.dot(desc[0], w_proj, preferred_element_type=jnp.float32).astype(jnp.bfloat16)[
        None
    ]
    group_rows = lax.all_gather(own_rows, "grp", axis=0, tiled=True)
    next_rows = from_behind(group_rows, "img", -1)
    window = jnp.concatenate([group_rows, next_rows], 0)
    live_count = pair_count[0]
    slots = window_slot(pair_list, column_index, columns, members)

    def visit(position, totals):
        first_slot = slots[position, 0]
        second_slot = slots[position, 1]
        first_rows = lax.dynamic_index_in_dim(window, first_slot, 0, keepdims=False)
        second_rows = lax.dynamic_index_in_dim(window, second_slot, 0, keepdims=False)
        to_first, to_second = pair_messages(first_rows, second_rows)
        totals = totals.at[first_slot].add(to_first.astype(jnp.float32))
        return totals.at[second_slot].add(to_second.astype(jnp.float32))

    totals = jnp.zeros((2 * members, keypoints, D), jnp.float32)
    totals = lax.fori_loop(0, live_count, visit, totals)
    returned = from_behind(totals[members:], "img", 1)
    summed = lax.psum_scatter(totals[:members] + returned, "grp", scatter_dimension=0, tiled=True)
    message = summed[0].astype(jnp.bfloat16)
    update = jnp.dot(message, w_out, preferred_element_type=jnp.float32)
    return (desc[0].astype(jnp.float32) + update).astype(jnp.bfloat16)[None]


def solution(mesh):
    return jax.shard_map(
        on_device,
        mesh=mesh,
        in_specs=(
            P(("img", "grp"), None, None),
            P(),
            P(),
            P(("img", "grp"), None),
            P(("img", "grp")),
        ),
        out_specs=P(("img", "grp"), None, None),
        check_vma=False,
    )
```

profile of v0, /device:TPU:1, one launch (start us, length us, event | category | flops | bytes accessed | tf_op | source)
XLA Modules:
  0.0 399.2 jit_solution(12478828602547499768)
XLA Ops:
  6.5 0.9 copy-done
  7.5 2.5 convolution_convert_fusion
  10.0 54.8 %all-gather.3.cloned.1.call-done = bf16[4096,512]{1,0:T(8,128)(2,1)} async-done(((bf16[1024,512]{1,0:T(8,128)(2,1)}), bf16[4096,512]{1,0:T(8,128)(2,1)}) %all-gather.3.cloned.1.call-update) | async-done | bytes 4194320 | tf_op jit(solution)/shard_map/all_gather | solution.py:57
  66.2 47.0 %collective-permute-done = bf16[4,1024,512]{2,1,0:T(8,128)(2,1)} collective-permute-done((bf16[4,1024,512]{2,1,0:T(8,128)(2,1)}, bf16[4,1024,512]{2,1,0:T(8,128)(2,1)}, u32[]{:S(2)}, u32[]{:S(2)}) %collective-permute-start) | collective-permute-done | bytes 4194336 | tf_op jit(solution)/shard_map/ppermute | solution.py:14
  113.1 7.4 %pad_maximum_fusion = bf16[8,1024,512]{2,1,0:T(8,128)(2,1)} fusion(bf16[4,1024,512]{2,1,0:T(8,128)(2,1)} %collective-permute-done, bf16[4,1024,512]{2,1,0:T(8,128)(2,1)} %bitcast.64), kind=kLoop, calls=%fused_computation.98 | loop fusion | flops 4194304 | bytes 16777216 | tf_op jit(solution)/shard_map/concatenate | solution.py:59
  120.5 4.3 %broadcast_in_dim.6 = f32[8,1024,256]{1,2,0:T(8,128)} broadcast(f32[]{:T(128)} %constant.102.clone.1), dimensions={} | broadcast | bytes 8388612 | tf_op jit(solution)/shard_map/broadcast_in_dim | solution.py:72
  124.8 65.9 %while.12 = (s32[]{:T(128)}, f32[8,1024,256]{1,2,0:T(8,128)}, s32[]{:T(128)}, s32[5,2]{0,1:T(2,128)S(1)}, bf16[8,1024,512]{2,1,0:T(8,128)(2,1)}, /*index=5*/s32[...) while((s32[]{:T(128)}, f32[8,1024,256]{1,2,0:T(8,128)}, s32[]{:T(128)}, ...), condition=%wide.region_19.20_spmd, body=%wide.region_0.19_spmd.sunk | while | flops 1683472384 | bytes 81955088 | solution.py:73
  131.0 1.7 dynamic-slice_bitcast_fusion.3
  133.5 1.6 fusion.108
  135.0 1.3 fusion.109
  136.3 1.0 fusion.114
  137.3 0.9 multiply_reduce_fusion.14
  138.2 1.6 fusion.106
  139.7 1.2 fusion.107
  141.0 1.0 fusion.113
  142.0 0.8 multiply_reduce_fusion.13
  142.8 1.6 fusion.104
  144.3 1.2 fusion.105
  145.6 1.0 fusion.112
  146.6 0.9 multiply_reduce_fusion.12
  147.4 1.6 fusion.102
  149.0 1.0 fusion.111
  150.0 1.2 fusion.103
  151.3 3.0 fusion.110
  154.3 3.1 fusion.115
  163.5 1.7 dynamic-slice_bitcast_fusion.3
  165.9 1.6 fusion.108
  167.5 1.3 fusion.109
  168.7 1.0 fusion.114
  169.7 0.9 multiply_reduce_fusion.14
  170.6 1.6 fusion.106
  172.2 1.2 fusion.107
  173.4 1.0 fusion.113
  174.4 0.8 multiply_reduce_fusion.13
  175.2 1.6 fusion.104
  176.8 1.2 fusion.105
  178.0 1.0 fusion.112
  179.0 0.9 multiply_reduce_fusion.12
  179.9 1.6 fusion.102
  181.5 1.0 fusion.111
  182.5 1.2 fusion.103
  183.7 3.0 fusion.110
  186.8 3.1 fusion.115
  190.8 2.7 slice.93
  193.5 45.4 %collective-permute-done.1 = f32[4,1024,256]{1,2,0:T(8,128)S(1)} collective-permute-done((f32[4,1024,256]{1,2,0:T(8,128)S(1)}, f32[4,1024,256]{1,2,0:T(8,128)S(1)}, u32[]{:S(2)}, u32[]{:S(2)}) %collective-permute-start.1) | collective-permute-done | bytes 4194336 | tf_op jit(solution)/shard_map/ppermute | solution.py:14
  239.0 2.9 slice_add_fusion
  241.8 148.2 %reduce-scatter.2.cloned.1.call-done = f32[1,1024,256]{1,2,0:T(8,128)} async-done(((f32[4,1024,256]{1,2,0:T(8,128)}), f32[1,1024,256]{1,2,0:T(8,128)}) %reduce-scatter.2.cloned.1.call-update) | async-done | bytes 1048592 | tf_op jit(solution)/shard_map/reduce_scatter | solution.py:75
  390.0 2.4 fusion.63
  (22 shorter events, 6.0 us)
Async XLA Ops:
  6.5 1.0 copy-start
  6.5 58.2 %all-gather.3.cloned.1.call-start = ((), (), s32[]{:S(2)}) async-start(), calls=%async_computation.2 | async-start | bytes 5242880 | tf_op jit(solution)/shard_map/all_gather | solution.py:57
  10.0 380.1 %reduce-scatter.2.cloned.1.call-start = ((), (), s32[]{:S(2)}) async-start(), calls=%async_computation.1 | async-start | bytes 5242880 | tf_op jit(solution)/shard_map/reduce_scatter | solution.py:75
  64.8 48.3 %collective-permute-start = (bf16[4,1024,512]{2,1,0:T(8,128)(2,1)}, bf16[4,1024,512]{2,1,0:T(8,128)(2,1)}, u32[]{:S(2)}, u32[]{:S(2)}) collective-permute-start(bf16[4,1024,512]{2,1,0:T(8,128)(2,1)} %bitcast.63), channel_id=1, source_target_pairs={{4,0},{8,4},{12,8},{16,12},{20,16},{24,20},{28,24},{32,28},{36,32}... | collective-permute-start | bytes 12582920 | tf_op jit(solution)/shard_map/ppermute | solution.py:14
  120.5 4.3 %copy-start.4 = (s32[3]{0:T(128)S(1)}, s32[3]{0:T(128)}, u32[]{:S(2)}) copy-start(s32[3]{0:T(128)} %constant.96.clone.1) | copy-start | bytes 40
  190.8 48.2 %copy-start.1 = (f32[8,1024,256]{1,2,0:T(8,128)S(1)}, f32[8,1024,256]{1,2,0:T(8,128)}, u32[]{:S(2)}) copy-start(f32[8,1024,256]{1,2,0:T(8,128)} %get-tuple-element.57) | copy-start | bytes 25165828
  193.4 45.5 %collective-permute-start.1 = (f32[4,1024,256]{1,2,0:T(8,128)S(1)}, f32[4,1024,256]{1,2,0:T(8,128)S(1)}, u32[]{:S(2)}, u32[]{:S(2)}) collective-permute-start(f32[4,1024,256]{1,2,0:T(8,128)S(1)} %slice.93), channel_id=1, source_target_pairs={{252,0},{0,4},{4,8},{8,12},{12,16},{16,20},{20,24},{24,28},{28,32}... | collective-permute-start | bytes 12582920 | tf_op jit(solution)/shard_map/ppermute | solution.py:14
  241.8 148.2 %copy-start.2 = (bf16[1,1024,256]{2,1,0:T(8,128)(2,1)S(1)}, bf16[1,1024,256]{2,1,0:T(8,128)(2,1)}, u32[]{:S(2)}) copy-start(bf16[1,1024,256]{2,1,0:T(8,128)(2,1)} %param.11) | copy-start | bytes 1572868
  241.8 148.2 %copy-start.3 = (bf16[256,256]{1,0:T(8,128)(2,1)S(1)}, bf16[256,256]{1,0:T(8,128)(2,1)}, u32[]{:S(2)}) copy-start(bf16[256,256]{1,0:T(8,128)(2,1)} %param.13) | copy-start | bytes 393220
Sparse Core Ops, SparseCore 0:
  10.1 54.6 all-gather.2
  242.0 148.0 reduce-scatter.1
where the time goes:
time: 400 us; the launch traced here: 399 us
  waiting for transfers between devices  295 us (74%)
  other arithmetic  37.2 us (9%)
  matrix products  29.6 us (7%)
  between operations  13.4 us (3%)
  local copies, waits for them, and re-layouts  12.6 us (3%)
  loops' own time  10.2 us (3%)
    reduce_scatter x1, waiting for transfers between devices, on_device(): lax.psum_scatter(totals[:members] + returned, 'grp', scatter_dimension=0,...  148 us
    ppermute x2, waiting for transfers between devices, from_behind(): return lax.ppermute(block, axis, route)  92.4 us
    all_gather x1, waiting for transfers between devices, on_device(): group_rows = lax.all_gather(own_rows, 'grp', axis=0, tiled=True)  54.8 us
    reduce_sum x8, other arithmetic, pair_messages(): jnp.sum(downward, axis=0, keepdims=True)  12.4 us
    another operation x1, loops' own time, on_device(): totals = lax.fori_loop(0, live_count, visit, totals)  10.2 us
    dot_general x8, matrix products, pair_messages(): jnp.dot(across, value_second, preferred_element_type=jnp.float32)  9.98 us
    dot_general x8, matrix products, pair_messages(): lax.dot_general(downward, value_first, (((0,), (0,)), ((), ())), preferre...  8.13 us
  transfers between devices with their start and end apart: 4, of which 4 were waited for; matrix products, arithmetic and copies ran while one was open for 0% of the time, Pallas kernels for 0%

commit v1 on v0

--- a/solution.py
+++ b/solution.py
@@ -54,7 +54,12 @@
     own_rows = jnp.dot(desc[0], w_proj, preferred_element_type=jnp.float32).astype(jnp.bfloat16)[
         None
     ]
-    group_rows = lax.all_gather(own_rows, "grp", axis=0, tiled=True)
+    ring = [own_rows]
+    for hop in range(3):
+        ring.append(lax.ppermute(ring[-1], "grp", [(dev, (dev + 1) % 4) for dev in range(4)]))
+    group_rows = jnp.roll(
+        jnp.concatenate(ring[::-1], axis=0), (lax.axis_index("grp") + 1) * ring[0].shape[0], axis=0
+    )
     next_rows = from_behind(group_rows, "img", -1)
     window = jnp.concatenate([group_rows, next_rows], 0)
     live_count = pair_count[0]

time: 400 us -> 428 us (1.070)
  waiting for transfers between devices: 295 us -> 310 us
  starting transfers between devices: 0.8 us -> 9.33 us
  local copies, waits for them, and re-layouts: 12.6 us -> 17.8 us
    ppermute x0 -> x3, waiting for transfers between devices: none -> 65.8 us  [on_device(): lax.ppermute(ring[-1], 'grp', [(dev, (dev + 1) % 4) for dev in range(4)])]
    all_gather x1 -> x0, waiting for transfers between devices: 54.8 us -> none  [on_device(): group_rows = lax.all_gather(own_rows, 'grp', axis=0, tiled=True)]
    ppermute x0 -> x3, starting transfers between devices: none -> 4.64 us  [on_device(): lax.ppermute(ring[-1], 'grp', [(dev, (dev + 1) % 4) for dev in range(4)])]
  transfers between devices with their start and end apart: 4 -> 6, of which waited for: 4 -> 6; matrix products, arithmetic and copies ran while one was open for 0% -> 0% of each run, Pallas kernels for 0% -> 0%
where the time goes in v1:
time: 428 us; the launch traced here: 426 us
  waiting for transfers between devices  310 us (72%)
  other arithmetic  36.6 us (9%)
  matrix products  28.6 us (7%)
  local copies, waits for them, and re-layouts  17.8 us (4%)
  between operations  13.5 us (3%)
  loops' own time  10.2 us (2%)
  starting transfers between devices  9.33 us (2%)
    reduce_scatter x1, waiting for transfers between devices, on_device(): lax.psum_scatter(totals[:members] + returned, 'grp', scatter_dimension=0,...  149 us
    ppermute x2, waiting for transfers between devices, from_behind(): return lax.ppermute(block, axis, route)  96 us
    ppermute x3, waiting for transfers between devices, on_device(): lax.ppermute(ring[-1], 'grp', [(dev, (dev + 1) % 4) for dev in range(4)])  65.8 us
    reduce_sum x8, other arithmetic, pair_messages(): jnp.sum(downward, axis=0, keepdims=True)  12.4 us
    another operation x1, loops' own time, on_device(): totals = lax.fori_loop(0, live_count, visit, totals)  10.2 us
    dot_general x8, matrix products, pair_messages(): jnp.dot(across, value_second, preferred_element_type=jnp.float32)  9.98 us
  transfers between devices with their start and end apart: 6, of which 6 were waited for; matrix products, arithmetic and copies ran while one was open for 0% of the time, Pallas kernels for 0%

profile of v1, /device:TPU:1, one launch (start us, length us, event | category | flops | bytes accessed | tf_op | source)
XLA Modules:
  0.0 426.4 jit_solution(13537211583850164748)
XLA Ops:
  7.5 1.5 fusion.62
  9.0 2.2 collective-permute-start
  11.2 22.3 %collective-permute-done = bf16[1,1024,512]{2,1,0:T(8,128)(2,1)S(1)} collective-permute-done((bf16[1,1024,512]{2,1,0:T(8,128)(2,1)S(1)}, bf16[1,1024,512]{2,1,0:T(8,128)(2,1)S(1)}, u32[]{:S(2)}, u32[]{:S(2)}) %collective-permute-start) | collective-permute-done | bytes 1048608 | tf_op jit(solution)/shard_map/ppermute | solution.py:59
  33.5 1.6 collective-permute-start.1
  35.0 22.0 %collective-permute-done.1 = bf16[1,1024,512]{2,1,0:T(8,128)(2,1)S(1)} collective-permute-done((bf16[1,1024,512]{2,1,0:T(8,128)(2,1)S(1)}, bf16[1,1024,512]{2,1,0:T(8,128)(2,1)S(1)}, u32[]{:S(2)}, u32[]{:S(2)}) %collective-permute-start.1) | collective-permute-done | bytes 1048608 | tf_op jit(solution)/shard_map/ppermute | solution.py:59
  57.9 21.4 %collective-permute-done.2 = bf16[1,1024,512]{2,1,0:T(8,128)(2,1)} collective-permute-done((bf16[1,1024,512]{2,1,0:T(8,128)(2,1)S(1)}, bf16[1,1024,512]{2,1,0:T(8,128)(2,1)}, u32[]{:S(2)}, u32[]{:S(2)}) %collective-permute-start.2) | collective-permute-done | bytes 1048608 | tf_op jit(solution)/shard_map/ppermute | solution.py:59
  79.4 1.3 constant_dynamic-update-slice_fusion.7
  80.9 1.3 constant_dynamic-update-slice_fusion.3
  82.4 2.3 constant_dynamic-slice_fusion.2
  84.7 4.6 %collective-permute-start.3 = (bf16[4,1024,512]{2,1,0:T(8,128)(2,1)}, bf16[4,1024,512]{2,1,0:T(8,128)(2,1)}, u32[]{:S(2)}, u32[]{:S(2)}) collective-permute-start(bf16[4,1024,512]{2,1,0:T(8,128)(2,1)} %constant_dynamic-slice_fusion.2), channel_id=1, source_target_pairs={{4,0},{8,4},{12,8},{16,12},{20,16},{24,20},{28,24},{32,28},{36,32}... | collective-permute-start | bytes 12582920 | tf_op jit(solution)/shard_map/ppermute | solution.py:14
  89.3 50.5 %collective-permute-done.3 = bf16[4,1024,512]{2,1,0:T(8,128)(2,1)} collective-permute-done((bf16[4,1024,512]{2,1,0:T(8,128)(2,1)}, bf16[4,1024,512]{2,1,0:T(8,128)(2,1)}, u32[]{:S(2)}, u32[]{:S(2)}) %collective-permute-start.3) | collective-permute-done | bytes 4194336 | tf_op jit(solution)/shard_map/ppermute | solution.py:14
  139.8 7.4 %pad_maximum_fusion = bf16[8,1024,512]{2,1,0:T(8,128)(2,1)} fusion(bf16[4,1024,512]{2,1,0:T(8,128)(2,1)} %collective-permute-done.3, bf16[4,1024,512]{2,1,0:T(8,128)(2,1)} %constant_dynamic-slice_fusion.2), kind=kLoop, calls=%fused_computation.98 | loop fusion | flops 4194304 | bytes 16777216 | tf_op jit(solution)/shard_map/concatenate | solution.py:64
  147.3 4.3 %broadcast_in_dim.6 = f32[8,1024,256]{1,2,0:T(8,128)} broadcast(f32[]{:T(128)} %constant.120.clone.1), dimensions={} | broadcast | bytes 8388612 | tf_op jit(solution)/shard_map/broadcast_in_dim | solution.py:77
  151.5 65.9 %while.12 = (s32[]{:T(128)}, f32[8,1024,256]{1,2,0:T(8,128)}, s32[]{:T(128)}, s32[5,2]{0,1:T(2,128)S(1)}, bf16[8,1024,512]{2,1,0:T(8,128)(2,1)}, /*index=5*/s32[...) while((s32[]{:T(128)}, f32[8,1024,256]{1,2,0:T(8,128)}, s32[]{:T(128)}, ...), condition=%wide.region_19.20_spmd, body=%wide.region_0.19_spmd.sunk | while | flops 1683472384 | bytes 81955088 | solution.py:78
  157.7 1.7 dynamic-slice_bitcast_fusion.3
  160.2 1.6 fusion.109
  161.8 1.2 fusion.110
  163.0 1.0 fusion.115
  164.9 1.6 fusion.107
  166.4 1.2 fusion.108
  167.7 1.0 fusion.114
  169.5 1.6 fusion.105
  171.1 1.2 fusion.106
  172.3 1.0 fusion.113
  174.2 1.6 fusion.103
  175.7 1.0 fusion.112
  176.8 1.2 fusion.104
  178.0 3.0 fusion.111
  181.0 3.1 fusion.116
  190.2 1.7 dynamic-slice_bitcast_fusion.3
  192.6 1.6 fusion.109
  194.2 1.2 fusion.110
  195.4 1.0 fusion.115
  197.3 1.6 fusion.107
  198.9 1.2 fusion.108
  200.1 1.0 fusion.114
  201.9 1.6 fusion.105
  203.5 1.2 fusion.106
  206.6 1.6 fusion.103
  208.2 1.0 fusion.112
  209.2 1.2 fusion.104
  210.5 3.0 fusion.111
  213.5 3.1 fusion.116
  217.5 2.7 slice.93
  220.2 45.4 %collective-permute-done.4 = f32[4,1024,256]{1,2,0:T(8,128)S(1)} collective-permute-done((f32[4,1024,256]{1,2,0:T(8,128)S(1)}, f32[4,1024,256]{1,2,0:T(8,128)S(1)}, u32[]{:S(2)}, u32[]{:S(2)}) %collective-permute-start.4) | collective-permute-done | bytes 4194336 | tf_op jit(solution)/shard_map/ppermute | solution.py:14
  265.7 2.9 slice_add_fusion
  268.6 148.6 %reduce-scatter.2.cloned.1.call-done = f32[1,1024,256]{1,2,0:T(8,128)} async-done(((f32[4,1024,256]{1,2,0:T(8,128)}), f32[1,1024,256]{1,2,0:T(8,128)}) %reduce-scatter.2.cloned.1.call-update) | async-done | bytes 1048592 | tf_op jit(solution)/shard_map/reduce_scatter | solution.py:80
  417.2 2.4 fusion.64
  (38 shorter events, 12.9 us)
Async XLA Ops:
  6.5 1.0 copy-start
  6.5 410.6 %reduce-scatter.2.cloned.1.call-start = ((), (), s32[]{:S(2)}) async-start(), calls=%async_computation.1 | async-start | bytes 5242880 | tf_op jit(solution)/shard_map/reduce_scatter | solution.py:80
  9.0 24.5 %collective-permute-start = (bf16[1,1024,512]{2,1,0:T(8,128)(2,1)S(1)}, bf16[1,1024,512]{2,1,0:T(8,128)(2,1)S(1)}, u32[]{:S(2)}, u32[]{:S(2)}) collective-permute-start(bf16[1,1024,512]{2,1,0:T(8,128)(2,1)S(1)} %fusion.62), channel_id=1, source_target_pairs={{0,1},{1,2},{2,3},{3,0},{4,5},{5,6},{6,7},{7,4},{8,9},{9,10},{10,1... | collective-permute-start | bytes 3145736 | tf_op jit(solution)/shard_map/ppermute | solution.py:59
  33.5 23.6 %collective-permute-start.1 = (bf16[1,1024,512]{2,1,0:T(8,128)(2,1)S(1)}, bf16[1,1024,512]{2,1,0:T(8,128)(2,1)S(1)}, u32[]{:S(2)}, u32[]{:S(2)}) collective-permute-start(bf16[1,1024,512]{2,1,0:T(8,128)(2,1)S(1)} %collective-permute-done), channel_id=1, source_target_pairs={{0,1},{1,2},{2,3},{3,0},{4,5},{5,6},{6,7},{7,4},{8,9},{9,10},{10,1... | collective-permute-start | bytes 3145736 | tf_op jit(solution)/shard_map/ppermute | solution.py:59
  57.1 22.3 %collective-permute-start.2 = (bf16[1,1024,512]{2,1,0:T(8,128)(2,1)S(1)}, bf16[1,1024,512]{2,1,0:T(8,128)(2,1)}, u32[]{:S(2)}, u32[]{:S(2)}) collective-permute-start(bf16[1,1024,512]{2,1,0:T(8,128)(2,1)S(1)} %collective-permute-done.1), channel_id=1, source_target_pairs={{0,1},{1,2},{2,3},{3,0},{4,5},{5,6},{6,7},{7,4},{8,9},{9,10},{10,1... | collective-permute-start | bytes 3145736 | tf_op jit(solution)/shard_map/ppermute | solution.py:59
  82.4 6.9 %copy-start.6 = (s32[5,2]{0,1:T(2,128)S(1)}, s32[5,2]{0,1:T(2,128)}, u32[]{:S(2)}) copy-start(s32[5,2]{0,1:T(2,128)} %param.14) | copy-start | bytes 124
  84.7 55.2 %collective-permute-start.3 = (bf16[4,1024,512]{2,1,0:T(8,128)(2,1)}, bf16[4,1024,512]{2,1,0:T(8,128)(2,1)}, u32[]{:S(2)}, u32[]{:S(2)}) collective-permute-start(bf16[4,1024,512]{2,1,0:T(8,128)(2,1)} %constant_dynamic-slice_fusion.2), channel_id=1, source_target_pairs={{4,0},{8,4},{12,8},{16,12},{20,16},{24,20},{28,24},{32,28},{36,32}... | collective-permute-start | bytes 12582920 | tf_op jit(solution)/shard_map/ppermute | solution.py:14
  147.3 4.3 %copy-start.5 = (s32[3]{0:T(128)S(1)}, s32[3]{0:T(128)}, u32[]{:S(2)}) copy-start(s32[3]{0:T(128)} %constant.114.clone.1) | copy-start | bytes 40
  217.5 48.2 %copy-start.2 = (f32[8,1024,256]{1,2,0:T(8,128)S(1)}, f32[8,1024,256]{1,2,0:T(8,128)}, u32[]{:S(2)}) copy-start(f32[8,1024,256]{1,2,0:T(8,128)} %get-tuple-element.57) | copy-start | bytes 25165828
  220.1 45.5 %collective-permute-start.4 = (f32[4,1024,256]{1,2,0:T(8,128)S(1)}, f32[4,1024,256]{1,2,0:T(8,128)S(1)}, u32[]{:S(2)}, u32[]{:S(2)}) collective-permute-start(f32[4,1024,256]{1,2,0:T(8,128)S(1)} %slice.93), channel_id=1, source_target_pairs={{252,0},{0,4},{4,8},{8,12},{12,16},{16,20},{20,24},{24,28},{28,32}... | collective-permute-start | bytes 12582920 | tf_op jit(solution)/shard_map/ppermute | solution.py:14
  265.7 153.9 %copy-start.1 = (bf16[256,512]{1,0:T(8,128)(2,1)S(1)}, bf16[256,512]{1,0:T(8,128)(2,1)}, u32[]{:S(2)}) copy-start(bf16[256,512]{1,0:T(8,128)(2,1)} %param.12) | copy-start | bytes 786436
  268.5 148.7 %copy-start.3 = (bf16[1,1024,256]{2,1,0:T(8,128)(2,1)S(1)}, bf16[1,1024,256]{2,1,0:T(8,128)(2,1)}, u32[]{:S(2)}) copy-start(bf16[1,1024,256]{2,1,0:T(8,128)(2,1)} %param.11) | copy-start | bytes 1572868
  268.5 148.7 %copy-start.4 = (bf16[256,256]{1,0:T(8,128)(2,1)S(1)}, bf16[256,256]{1,0:T(8,128)(2,1)}, u32[]{:S(2)}) copy-start(bf16[256,256]{1,0:T(8,128)(2,1)} %param.13) | copy-start | bytes 393220
Sparse Core Ops, SparseCore 0:
  268.7 148.4 reduce-scatter.1
